TPU v7x, 32 devices: a whole 2x2x4 slice. The times are simulated.
32 devices in a mesh: seq: 8 (over z, x), head: 4 (over y, core).
Axes of the slice: x: 2, y: 2, z: 4, core: 2. Of those that a mesh axis runs over, the one named last changes fastest.
Arguments:
- h_in: float32 [2048, 1024], P('seq', 'head'), may hold values from -6 to 6
- norm_gain: float32 [2, 1024], P(None, 'head'), may hold values from 0.5 to 1.5
- w_z: bfloat16 [2, 1024, 2048], P(None, None, 'head'), may hold values from -0.1875 to 0.1875
- w_x: bfloat16 [2, 1024, 2048], P(None, None, 'head'), may hold values from -0.1875 to 0.1875
- w_bc: bfloat16 [2, 1024, 256], replicated, may hold values from -0.1875 to 0.1875
- w_dt: bfloat16 [2, 1024, 32], P(None, None, 'head'), may hold values from -0.1875 to 0.1875
- conv_x_w: float32 [2, 4, 2048], P(None, None, 'head'), may hold values from -3 to 3
- conv_x_b: float32 [2, 2048], P(None, 'head'), may hold values from -0.5 to 0.5
- conv_bc_w: float32 [2, 4, 256], replicated, may hold values from -3 to 3
- conv_bc_b: float32 [2, 256], replicated, may hold values from -0.5 to 0.5
- dt_bias: float32 [2, 32], P(None, 'head'), may hold values from -4 to -1
- a_log: float32 [2, 32], P(None, 'head'), may hold values from -10 to -1
- skip: float32 [2, 32], P(None, 'head'), may hold values from 0.5 to 1.5
- gate_gain: float32 [2, 2048], P(None, 'head'), may hold values from 0.5 to 1.5
- w_out: bfloat16 [2, 2048, 1024], P(None, 'head'), may hold values from -0.125 to 0.125
- d_out: float32 [2048, 1024], P('seq', 'head'), may hold values from -6 to 6
Outputs:
- h_out: float32 [2048, 1024], P('seq', 'head')
- d_h: float32 [2048, 1024], P('seq', 'head')
- d_norm_gain: float32 [2, 1024], P(None, 'head')
- d_w_z: float32 [2, 1024, 2048], P(None, 'seq', 'head')
- d_w_x: float32 [2, 1024, 2048], P(None, 'seq', 'head')
- d_w_bc: float32 [2, 1024, 256], replicated
- d_w_dt: float32 [2, 1024, 32], P(None, 'seq', 'head')
- d_conv_x_w: float32 [2, 4, 2048], P(None, None, 'head')
- d_conv_x_b: float32 [2, 2048], P(None, 'head')
- d_conv_bc_w: float32 [2, 4, 256], replicated
- d_conv_bc_b: float32 [2, 256], replicated
- d_dt_bias: float32 [2, 32], P(None, 'head')
- d_a_log: float32 [2, 32], P(None, 'head')
- d_skip: float32 [2, 32], P(None, 'head')
- d_gate_gain: float32 [2, 2048], P(None, 'head')
- d_w_out: float32 [2, 2048, 1024], P(None, 'head', 'seq')
All inputs are finite; a program needn't handle non-finite values.
Results may differ from a plain program's by a relative error of at most 0.014.
The roundings to bfloat16 on the way count: a program that leaves them out, or rounds other values in their place, can miss the bound.
Values may be sent and summed in bfloat16 or wider, within the bound.
A program may use at most 128 MiB of HBM per device.

v0:
```python
import jax
import jax.numpy as jnp
from jax import lax
from jax.sharding import PartitionSpec as P

D = 1024
HEAD_DIM = 64
STATE = 128
CONV = 4
SPAN = 256
LAYERS = 2
DI = 2048
epsilon = 1e-05
highest = lax.Precision.HIGHEST


def shifted(value, axis, steps):
    count = lax.axis_size(axis)
    first, last = (max(0, -steps), min(count, count - steps))
    return lax.ppermute(value, axis, [(source, source + steps) for source in range(first, last)])


def entering_2(value, axis, join, neutral, backward):
    count, mine = (lax.axis_size(axis), lax.axis_index(axis))
    pieces = jax.tree.map(lambda part: lax.all_gather(part, axis), value)
    if backward:
        pieces = jax.tree.map(lambda part: part[::-1], pieces)
        mine = count - 1 - mine
    total = jax.tree.map(
        lambda part, zero: jnp.full_like(part, 0) + jnp.asarray(zero, part.dtype), value, neutral
    )

    def lap(position, total):
        longer = join(total, jax.tree.map(lambda part: part[position], pieces))
        return jax.tree.map(lambda new, old: jnp.where(position < mine, new, old), longer, total)

    return lax.fori_loop(0, count - 1, lap, total)


def conv_inputs(extended, dt_raw, conv_weight, conv_bias, dt_bias, a_log):
    row_count = dt_raw.shape[0]
    mixed = jnp.zeros((row_count, extended.shape[1]), jnp.float32) + conv_bias[None, :]
    for offset in range(CONV):
        mixed = mixed + conv_weight[offset][None, :] * extended[offset : offset + row_count]
    active = jax.nn.silu(mixed)
    inner = extended.shape[1] - 2 * STATE
    head_count = dt_raw.shape[1]
    values = active[:, :inner].reshape(row_count, head_count, HEAD_DIM)
    b_proj = active[:, inner : inner + STATE]
    c_proj = active[:, inner + STATE :]
    steps_dt = jax.nn.softplus(dt_raw + dt_bias[None, :])
    log_decay = -steps_dt * jnp.exp(a_log)[None, :]
    return (values, b_proj, c_proj, steps_dt, log_decay)


def scan_from_zero(values, b_proj, c_proj, steps_dt, log_decay):
    row_count, head_count = steps_dt.shape
    blocks = row_count // SPAN
    causal = (jnp.arange(SPAN)[:, None] >= jnp.arange(SPAN)[None, :])[None]

    def one_block(carried, block_data):
        block_vals, b_blk, c_blk, dt_blk, la_blk = block_data
        cumulative = jnp.cumsum(la_blk, axis=0)
        cum_heads = cumulative.T
        spread = cum_heads[:, :, None] - cum_heads[:, None, :]
        weights = jnp.where(causal, jnp.exp(jnp.where(causal, spread, 0.0)), 0.0)
        scores = jnp.dot(c_blk, b_blk.T, precision=highest)
        scaled = block_vals * dt_blk[:, :, None]
        y_diag = jnp.einsum("htu,uhp->thp", weights * scores[None], scaled, precision=highest)
        y_off = (
            jnp.einsum("tn,hpn->thp", c_blk, carried, precision=highest)
            * jnp.exp(cumulative)[:, :, None]
        )
        ending = cumulative[-1]
        tail_decay = jnp.exp(ending[None, :] - cumulative)
        updated = carried * jnp.exp(ending)[:, None, None] + jnp.einsum(
            "uhp,un->hpn", scaled * tail_decay[:, :, None], b_blk, precision=highest
        )
        return (updated, y_diag + y_off)

    stacked = (
        values.reshape(blocks, SPAN, head_count, HEAD_DIM),
        b_proj.reshape(blocks, SPAN, STATE),
        c_proj.reshape(blocks, SPAN, STATE),
        steps_dt.reshape(blocks, SPAN, head_count),
        log_decay.reshape(blocks, SPAN, head_count),
    )
    initial = jnp.zeros((head_count, HEAD_DIM, STATE), jnp.float32)
    last_state, outputs = lax.scan(one_block, initial, stacked)
    return (outputs.reshape(row_count, head_count, HEAD_DIM), last_state)


def carry_term(c_proj, log_decay, entering):
    cumulative = jnp.cumsum(log_decay, axis=0)
    return (
        jnp.einsum("tn,hpn->thp", c_proj, entering, precision=highest)
        * jnp.exp(cumulative)[:, :, None]
    )


def link_states(earlier, later):
    return (earlier[0] * later[0], later[0][:, None, None] * earlier[1] + later[1])


def token_sums(partial_sums):
    return lax.psum(partial_sums, "head")


def contract_first(left, right):
    return lax.dot_general(
        left, right, (((0,), (0,)), ((), ())), preferred_element_type=jnp.float32
    )


def local(
    h_in,
    norm_gain,
    w_z,
    w_x,
    w_bc,
    w_dt,
    conv_x_w,
    conv_x_b,
    conv_bc_w,
    conv_bc_b,
    dt_bias,
    a_log,
    skip,
    gate_gain,
    w_out,
    d_out,
):
    row_count = h_in.shape[0]
    inner = w_x.shape[2]
    head_count = w_dt.shape[2]
    hidden = h_in
    kept = []
    for layer_idx in range(LAYERS):
        gain_one = norm_gain[layer_idx]
        full_hidden, full_gain = (
            lax.all_gather(hidden, "head", axis=1, tiled=True),
            lax.all_gather(gain_one, "head", axis=0, tiled=True),
        )
        factor = lax.rsqrt(jnp.mean(full_hidden * full_hidden, axis=1) + epsilon)
        normed = (full_hidden * factor[:, None] * full_gain[None, :]).astype(jnp.bfloat16)
        gate_in = jnp.dot(normed, w_z[layer_idx], preferred_element_type=jnp.float32)
        x_in = jnp.dot(normed, w_x[layer_idx], preferred_element_type=jnp.float32)
        bc_in = jnp.dot(normed, w_bc[layer_idx], preferred_element_type=jnp.float32)
        dt_raw = jnp.dot(normed, w_dt[layer_idx], preferred_element_type=jnp.float32)
        conv_in = jnp.concatenate([x_in, bc_in], axis=1)
        before = shifted(conv_in[row_count - (CONV - 1) :], "seq", 1)
        extended = jnp.concatenate([before, conv_in], axis=0)
        conv_weight = jnp.concatenate([conv_x_w[layer_idx], conv_bc_w[layer_idx]], axis=1)
        conv_bias = jnp.concatenate([conv_x_b[layer_idx], conv_bc_b[layer_idx]], axis=0)
        inputs, input_back = jax.vjp(
            conv_inputs,
            extended,
            dt_raw,
            conv_weight,
            conv_bias,
            dt_bias[layer_idx],
            a_log[layer_idx],
        )
        values, b_proj, c_proj, steps_dt, log_decay = inputs
        local_part, block_back = jax.vjp(
            scan_from_zero, values, b_proj, c_proj, steps_dt, log_decay
        )
        scanned, leaving = local_part
        decays = jnp.exp(jnp.sum(log_decay, axis=0))
        identity = (jnp.ones_like(decays), jnp.zeros_like(leaving))
        entering = entering_2((decays, leaving), "seq", link_states, identity, False)[1]
        carried_part, carry_back = jax.vjp(carry_term, c_proj, log_decay, entering)
        mixed = scanned + carried_part + skip[layer_idx][None, :, None] * values
        gate_act = jax.nn.silu(gate_in)
        gated = mixed.reshape(row_count, inner) * gate_act
        gate_factor = lax.rsqrt(token_sums(jnp.sum(gated * gated, axis=1)) / DI + epsilon)
        scaled = (gated * gate_factor[:, None] * gate_gain[layer_idx][None, :]).astype(jnp.bfloat16)
        out_weight = w_out[layer_idx]
        summed = lax.psum_scatter(
            contract_first(out_weight, scaled.T), "head", scatter_dimension=0, tiled=True
        )
        kept.append(
            (
                hidden,
                factor,
                normed,
                gate_in,
                gate_act,
                gated,
                gate_factor,
                scaled,
                mixed,
                values,
                decays,
                entering,
                input_back,
                block_back,
                carry_back,
            )
        )
        hidden = hidden + summed.T
    grad = d_out
    collected = [None] * LAYERS
    for layer_idx in reversed(range(LAYERS)):
        (
            layer_input,
            factor,
            normed,
            gate_in,
            gate_act,
            gated,
            gate_factor,
            scaled,
            mixed,
            values,
            decays,
            entering,
            input_back,
            block_back,
            carry_back,
        ) = kept[layer_idx]
        grad_b = grad.astype(jnp.bfloat16)
        out_weight = w_out[layer_idx]
        grad_cols = lax.all_gather(grad_b, "head", axis=1, tiled=True)
        d_part = lax.dot_general(
            grad_cols, out_weight, (((1,), (1,)), ((), ())), preferred_element_type=jnp.float32
        )
        d_cols = contract_first(scaled, grad_cols)
        normalized = gated * gate_factor[:, None]
        d_ggain = jnp.sum(d_part * normalized, axis=0)
        d_norm_in = d_part * gate_gain[layer_idx][None, :]
        along = token_sums(jnp.sum(d_norm_in * normalized, axis=1)) / DI
        d_gated = gate_factor[:, None] * (d_norm_in - normalized * along[:, None])
        sigma = jax.nn.sigmoid(gate_in)
        d_gate = d_gated * mixed.reshape(row_count, inner) * sigma * (1.0 + gate_in * (1.0 - sigma))
        d_mixed = (d_gated * gate_act).reshape(row_count, head_count, HEAD_DIM)
        d_skipped = jnp.sum(d_mixed * values, axis=(0, 2))
        d_c_carry, d_la_carry, d_entering = carry_back(d_mixed)
        back_identity = (jnp.ones_like(decays), jnp.zeros_like(d_entering))
        leaving_grad = entering_2((decays, d_entering), "seq", link_states, back_identity, True)[1]
        d_decays = jnp.sum(leaving_grad * entering, axis=(1, 2)) * decays
        d_values, d_b_proj, d_c_local, d_steps, d_la_local = block_back((d_mixed, leaving_grad))
        d_values = d_values + skip[layer_idx][None, :, None] * d_mixed
        d_inputs = (
            d_values,
            d_b_proj,
            d_c_carry + d_c_local,
            d_steps,
            d_la_carry + d_la_local + d_decays[None, :],
        )
        d_extended, d_dtraw, d_cweight, d_cbias, d_dtbias, d_alog = input_back(d_inputs)
        returned = shifted(d_extended[: CONV - 1], "seq", -1)
        d_conv = d_extended[CONV - 1 :] + jnp.pad(returned, ((row_count - (CONV - 1), 0), (0, 0)))
        d_gate_b = d_gate.astype(jnp.bfloat16)
        d_x_b = d_conv[:, :inner].astype(jnp.bfloat16)
        d_shared = d_conv[:, inner:]
        d_dt_b = d_dtraw.astype(jnp.bfloat16)
        d_wz = contract_first(normed, d_gate_b)
        d_wx = contract_first(normed, d_x_b)
        d_wdt = contract_first(normed, d_dt_b)
        d_wbc = lax.dot_general(
            normed.astype(jnp.float32), d_shared, (((0,), (0,)), ((), ())), precision=highest
        )
        wz_now = w_z[layer_idx]
        wx_now = w_x[layer_idx]
        wdt_now = w_dt[layer_idx]
        wbc_now = w_bc[layer_idx]

        def product(weight, grads):
            return lax.dot_general(
                weight, grads, (((1,), (1,)), ((), ())), preferred_element_type=jnp.float32
            )

        shared_rows = wbc_now.astype(jnp.float32)
        shared_term = lax.dot_general(
            shared_rows, d_shared, (((1,), (1,)), ((), ())), precision=highest
        )
        d_normed = lax.psum_scatter(
            product(wz_now, d_gate_b)
            + product(wx_now, d_x_b)
            + product(wdt_now, d_dt_b)
            + shared_term,
            "head",
            scatter_dimension=0,
            tiled=True,
        ).T
        centered = layer_input * factor[:, None]
        d_ngain = jnp.sum(d_normed * centered, axis=0)
        d_unit = d_normed * norm_gain[layer_idx][None, :]
        along_in = token_sums(jnp.sum(d_unit * centered, axis=1)) / D
        grad = grad + factor[:, None] * (d_unit - centered * along_in[:, None])
        collected[layer_idx] = (
            d_wz,
            d_wx,
            d_wdt,
            d_cols,
            d_ngain,
            d_cweight[:, :inner],
            d_cbias[:inner],
            d_ggain,
            d_dtbias,
            d_alog,
            d_skipped,
            d_wbc,
            d_cweight[:, inner:],
            d_cbias[inner:],
        )
    stacks = [
        jnp.stack([collected[layer_idx][member] for layer_idx in range(LAYERS)])
        for member in range(14)
    ]
    weight_sums = (
        lax.psum_scatter(
            stacks[0].astype(jnp.bfloat16), "seq", scatter_dimension=1, tiled=True
        ).astype(jnp.float32),
        lax.psum_scatter(
            stacks[1].astype(jnp.bfloat16), "seq", scatter_dimension=1, tiled=True
        ).astype(jnp.float32),
        lax.psum_scatter(
            stacks[2].astype(jnp.bfloat16), "seq", scatter_dimension=1, tiled=True
        ).astype(jnp.float32),
        lax.psum_scatter(
            stacks[3].astype(jnp.bfloat16), "seq", scatter_dimension=2, tiled=True
        ).astype(jnp.float32),
    )
    vector_sums = lax.psum(
        (stacks[4], stacks[5], stacks[6], stacks[7], stacks[8], stacks[9], stacks[10]), "seq"
    )
    shared_sums = lax.psum((stacks[11], stacks[12], stacks[13]), ("seq", "head"))
    return (
        hidden,
        grad,
        vector_sums[0],
        weight_sums[0],
        weight_sums[1],
        shared_sums[0],
        weight_sums[2],
        vector_sums[1],
        vector_sums[2],
        shared_sums[1],
        shared_sums[2],
        vector_sums[4],
        vector_sums[5],
        vector_sums[6],
        vector_sums[3],
        weight_sums[3],
    )


def solution(mesh):
    return jax.shard_map(
        local,
        mesh=mesh,
        in_specs=(
            P("seq", "head"),
            P(None, "head"),
            P(None, None, "head"),
            P(None, None, "head"),
            P(),
            P(None, None, "head"),
            P(None, None, "head"),
            P(None, "head"),
            P(),
            P(),
            P(None, "head"),
            P(None, "head"),
            P(None, "head"),
            P(None, "head"),
            P(None, "head", None),
            P("seq", "head"),
        ),
        out_specs=(
            P("seq", "head"),
            P("seq", "head"),
            P(None, "head"),
            P(None, "seq", "head"),
            P(None, "seq", "head"),
            P(),
            P(None, "seq", "head"),
            P(None, None, "head"),
            P(None, "head"),
            P(),
            P(),
            P(None, "head"),
            P(None, "head"),
            P(None, "head"),
            P(None, "head"),
            P(None, "head", "seq"),
        ),
        check_vma=False,
    )
```

profile of v0, /device:TPU:0, one launch (start us, length us, event | category | flops | bytes accessed | tf_op | source)
XLA Modules:
  0.0 995.1 jit_solution(10929443034664853142)
XLA Ops:
  8.7 6.0 all-gather
  22.1 6.9 all-gather.15.cloned.1.call-done
  45.5 21.2 %all-reduce.26 = f32[64]{0:T(128)S(1)} all-reduce(f32[64]{0:T(128)S(1)} %exponential_dynamic-update-slice_fusion.1), channel_id=3, replica_groups=mesh['seq'=8,'head'=4] {'seq'}, use_global_device_ids=true, to_apply=%add.26 | all-reduce | flops 64 | bytes 512
  68.5 23.3 %all-gather.19.cloned.1.call-done = f32[64,64,128]{2,1,0:T(8,128)} async-done(((f32[8,64,128]{2,1,0:T(8,128)}), f32[64,64,128]{2,1,0:T(8,128)}) %all-gather.19.cloned.1.call-update) | async-done | bytes 2097168 | tf_op jit(solution)/shard_map/all_gather | solution.py:25
  91.8 7.6 while.44
  109.1 5.8 psum.112
  117.8 23.7 %reduce-scatter.13.cloned.1.call-done = f32[256,256]{0,1:T(8,128)} async-done(((f32[1024,256]{0,1:T(8,128)}), f32[256,256]{0,1:T(8,128)}) %reduce-scatter.13.cloned.1.call-update) | async-done | bytes 262160 | tf_op jit(solution)/shard_map/reduce_scatter | solution.py:179
  149.6 10.6 %all-gather.17.cloned.1.call-done = f32[256,1024]{1,0:T(8,128)} async-done(((f32[256,256]{1,0:T(8,128)}), f32[256,1024]{1,0:T(8,128)}) %all-gather.17.cloned.1.call-update) | async-done | bytes 1048592 | tf_op jit(solution)/shard_map/all_gather | solution.py:141
  181.6 7.0 all_gather.64
  189.3 22.7 %all-reduce.27 = f32[64]{0:T(128)S(1)} all-reduce(f32[64]{0:T(128)S(1)} %exponential_dynamic-update-slice_fusion), channel_id=6, replica_groups=mesh['seq'=8,'head'=4] {'seq'}, use_global_device_ids=true, to_apply=%add.27 | all-reduce | flops 64 | bytes 512
  217.7 13.2 %all-gather.21.cloned.1.call-done = f32[64,64,128]{2,1,0:T(8,128)} async-done(((f32[8,64,128]{2,1,0:T(8,128)}), f32[64,64,128]{2,1,0:T(8,128)}) %all-gather.21.cloned.1.call-update) | async-done | bytes 2097168 | tf_op jit(solution)/shard_map/all_gather | solution.py:25
  230.9 15.9 %while.45 = (s32[]{:T(128)}, f32[8,64,128]{2,1,0:T(8,128)S(1)}, s32[]{:T(128)}, f32[8,8]{1,0:T(8,128)}, f32[8,8,64,128]{3,2,1,0:T(8,128)}, /*index=5*/s32[]{:T(128)}, s32[]{:T(128)}) while((s32[]{:T(128)}, f32[8,64,128]{2,1,0:T(8,128)S(1)}, s32[]{:T(128)}, f32[8,8]{1,0:T(8,128)}, f32[8,8,64,128]{3,2,1,0:T(8,128)}, ...), condition=%wide.region_14.16_spmd.clone, body=%wide.region_13.15_spmd.clone.sunk | while | flops 262148 | bytes 786633 | solution.py:37
  258.1 5.6 psum.113
  267.1 6.6 psum.114
  306.4 22.6 %all-gather.23.cloned.1.call-done = f32[64,64,128]{2,1,0:T(8,128)} async-done(((f32[8,64,128]{2,1,0:T(8,128)}), f32[64,64,128]{2,1,0:T(8,128)}) %all-gather.23.cloned.1.call-update) | async-done | bytes 2097168 | tf_op jit(solution)/shard_map/all_gather | solution.py:25
  332.1 15.8 %while.46 = (s32[]{:T(128)}, f32[8,64,128]{2,1,0:T(8,128)S(1)}, s32[]{:T(128)}, f32[8,8]{1,0:T(8,128)}, f32[8,8,64,128]{3,2,1,0:T(8,128)}, /*index=5*/s32[]{:T(128)}, s32[]{:T(128)}) while((s32[]{:T(128)}, f32[8,64,128]{2,1,0:T(8,128)S(1)}, s32[]{:T(128)}, f32[8,8]{1,0:T(8,128)}, f32[8,8,64,128]{3,2,1,0:T(8,128)}, ...), condition=%wide.region_22.24_spmd.clone, body=%wide.region_21.23_spmd.clone.sunk | while | flops 262148 | bytes 786633 | solution.py:37
  388.6 21.4 %reduce-scatter.17.cloned.1.call-done = f32[256,256]{0,1:T(8,128)} async-done(((f32[1024,256]{0,1:T(8,128)}), f32[256,256]{0,1:T(8,128)}) %reduce-scatter.17.cloned.1.call-update) | async-done | bytes 262160 | tf_op jit(solution)/shard_map/reduce_scatter | solution.py:278
  411.7 5.7 psum.115
  417.5 19.9 %reduce-scatter.15.cloned.1.call-done = f32[256,256]{0,1:T(8,128)} async-done(((f32[1024,256]{0,1:T(8,128)}), f32[256,256]{0,1:T(8,128)}) %reduce-scatter.15.cloned.1.call-update) | async-done | bytes 262160 | tf_op jit(solution)/shard_map/reduce_scatter | solution.py:179
  439.6 6.7 all_gather.67
  449.0 6.7 psum.116
  475.4 35.6 %all-gather.25.cloned.1.call-done = f32[64,64,128]{2,1,0:T(8,128)} async-done(((f32[8,64,128]{2,1,0:T(8,128)}), f32[64,64,128]{2,1,0:T(8,128)}) %all-gather.25.cloned.1.call-update) | async-done | bytes 2097168 | tf_op jit(solution)/shard_map/all_gather | solution.py:25
  514.2 12.3 %while.47 = (s32[]{:T(128)}, f32[8,64,128]{2,1,0:T(8,128)S(1)}, s32[]{:T(128)}, f32[8,8]{1,0:T(8,128)}, f32[8,8,64,128]{3,2,1,0:T(8,128)}, /*index=5*/s32[]{:T(128)}, s32[]{:T(128)}) while((s32[]{:T(128)}, f32[8,64,128]{2,1,0:T(8,128)S(1)}, s32[]{:T(128)}, f32[8,8]{1,0:T(8,128)}, f32[8,8,64,128]{3,2,1,0:T(8,128)}, ...), condition=%wide.region_43.45_spmd.clone, body=%wide.region_42.44_spmd.clone.sunk | while | flops 262148 | bytes 786633 | solution.py:37
  546.2 6.2 copy.152
  597.7 41.8 %all-reduce.28 = (f32[2,4,256]{2,1,0:T(4,128)}, f32[2,256]{1,0:T(2,128)}) all-reduce(f32[2,4,256]{2,1,0:T(4,128)S(1)} %pad_maximum_fusion.8, f32[2,256]{1,0:T(2,128)S(1)} %pad_maximum_fusion.16), channel_id=1, replica_groups=mesh['seq'=8,'head'=4] {'seq','head'}, use_global_device_ids=true, to_apply=%region_79.81 | all-reduce | flops 2560 | bytes 20480 | tf_op jit(solution)/shard_map/psum | solution.py:329
  643.6 31.7 %reduce-scatter.27.cloned.1.call-done = bf16[128,1024]{1,0:T(8,128)(2,1)} async-done(((bf16[1024,1024]{1,0:T(8,128)(2,1)}), bf16[128,1024]{1,0:T(8,128)(2,1)}) %reduce-scatter.27.cloned.1.call-update) | async-done | bytes 262160
  677.5 69.4 %reduce-scatter.21.cloned.1.call-done = bf16[2,128,512]{2,1,0:T(8,128)(2,1)} async-done(((bf16[2,1024,512]{2,1,0:T(8,128)(2,1)}), bf16[2,128,512]{2,1,0:T(8,128)(2,1)}) %reduce-scatter.21.cloned.1.call-update) | async-done | bytes 262160 | tf_op jit(solution)/shard_map/reduce_scatter | solution.py:313
  748.7 24.5 %reduce-scatter.19.cloned.1.call-done = f32[256,256]{0,1:T(8,128)} async-done(((f32[1024,256]{0,1:T(8,128)}), f32[256,256]{0,1:T(8,128)}) %reduce-scatter.19.cloned.1.call-update) | async-done | bytes 262160 | tf_op jit(solution)/shard_map/reduce_scatter | solution.py:278
  774.4 5.8 psum.117
  780.1 38.2 %all-reduce.29 = (f32[2,256]{1,0:T(2,128)}, f32[2,4,512]{2,1,0:T(4,128)}, f32[2,512]{1,0:T(2,128)}, f32[2,8]{1,0:T(2,128)}, f32[2,8]{1,0:T(2,128)}, /*index=5*/f32[2,8]{1,0:T(2,128)}, f32[2,512]{1,0:T(2,128)}) all-reduce(f32[2,256]{1,0:T(2,128)S(1)} %pad_maximum_fusion.15, ...), channel_id=1, replica_groups=mesh['seq'=8,'head'=4] {'seq'}, use_global_device_ids=true, to_apply=%region_62.64 | all-reduce | flops 6704 | bytes 53632 | tf_op jit(solution)/shard_map/psum | solution.py:326
  820.2 25.9 %reduce-scatter.23.cloned.1.call-done = bf16[2,128,512]{2,1,0:T(8,128)(2,1)} async-done(((bf16[2,1024,512]{2,1,0:T(8,128)(2,1)}), bf16[2,128,512]{2,1,0:T(8,128)(2,1)}) %reduce-scatter.23.cloned.1.call-update) | async-done | bytes 262160 | tf_op jit(solution)/shard_map/reduce_scatter | solution.py:316
  847.9 137.2 %all-reduce.32.cloned.1.call-done = f32[2,1024,256]{2,1,0:T(8,128)} async-done(((f32[2,1024,256]{2,1,0:T(8,128)}), f32[2,1024,256]{2,1,0:T(8,128)}) %all-reduce.32.cloned.1.call-update) | async-done | bytes 2097168 | tf_op jit(solution)/shard_map/psum | solution.py:329
  (630 shorter events, 325.7 us)
Async XLA Ops:
  7.2 21.8 %all-gather.15.cloned.1.call-start = ((), (), s32[]{:S(2)}) async-start(), calls=%async_computation.8 | async-start | bytes 1310720 | tf_op jit(solution)/shard_map/all_gather | solution.py:141
  7.9 83.9 %all-gather.19.cloned.1.call-start = ((), (), s32[]{:S(2)}) async-start(), calls=%async_computation.17 | async-start | bytes 2359296 | tf_op jit(solution)/shard_map/all_gather | solution.py:25
  8.7 134.5 %copy-start.103 = (f32[1,256]{1,0:T(1,128)}, f32[1,256]{1,0:T(1,128)S(1)}, u32[]{:S(2)}) copy-start(f32[1,256]{1,0:T(1,128)S(1)} %get-tuple-element.1312) | copy-start | bytes 3076
  32.9 6.0 collective-permute-start
  40.3 59.1 %copy-start = (f32[256,768]{1,0:T(8,128)}, f32[256,768]{1,0:T(8,128)S(1)}, u32[]{:S(2)}) copy-start(f32[256,768]{1,0:T(8,128)S(1)} %get-tuple-element.1275) | copy-start | bytes 2359300
  40.7 59.4 %copy-start.17 = (f32[256,512]{0,1:T(8,128)}, f32[256,512]{0,1:T(8,128)S(1)}, u32[]{:S(2)}) copy-start(f32[256,512]{0,1:T(8,128)S(1)} %copy.129) | copy-start | bytes 1572868
  42.3 99.1 %reduce-scatter.13.cloned.1.call-start = ((), (), s32[]{:S(2)}) async-start(), calls=%async_computation.9 | async-start | bytes 1310720 | tf_op jit(solution)/shard_map/reduce_scatter | solution.py:179
  44.8 55.2 %copy-start.134 = (f32[8]{0:T(128)}, f32[8]{0:T(128)S(1)}, u32[]{:S(2)}) copy-start(f32[8]{0:T(128)S(1)} %get-tuple-element.1317) | copy-start | bytes 100
  45.4 69.5 %copy-start.88 = (f32[1,512]{1,0:T(1,128)}, f32[1,512]{1,0:T(1,128)S(1)}, u32[]{:S(2)}) copy-start(f32[1,512]{1,0:T(1,128)S(1)} %get-tuple-element.1307) | copy-start | bytes 6148
  117.7 42.5 %all-gather.17.cloned.1.call-start = ((), (), s32[]{:S(2)}) async-start(), calls=%async_computation.10 | async-start | bytes 1310720 | tf_op jit(solution)/shard_map/all_gather | solution.py:141
  143.2 87.7 %all-gather.21.cloned.1.call-start = ((), (), s32[]{:S(2)}) async-start(), calls=%async_computation.18 | async-start | bytes 2359296 | tf_op jit(solution)/shard_map/all_gather | solution.py:25
  167.1 4.8 collective-permute-start.1
  180.5 148.4 %all-gather.23.cloned.1.call-start = ((), (), s32[]{:S(2)}) async-start(), calls=%async_computation.19 | async-start | bytes 2359296 | tf_op jit(solution)/shard_map/all_gather | solution.py:25
  281.6 128.5 %reduce-scatter.17.cloned.1.call-start = ((), (), s32[]{:S(2)}) async-start(), calls=%async_computation.12 | async-start | bytes 1310720 | tf_op jit(solution)/shard_map/reduce_scatter | solution.py:278
  376.8 5.6 collective-permute-start.2
  385.7 51.7 %reduce-scatter.15.cloned.1.call-start = ((), (), s32[]{:S(2)}) async-start(), calls=%async_computation.11 | async-start | bytes 1310720 | tf_op jit(solution)/shard_map/reduce_scatter | solution.py:179
  388.5 58.5 %copy-start.23 = (f32[256,512]{1,0:T(8,128)S(1)}, f32[256,512]{1,0:T(8,128)}, u32[]{:S(2)}) copy-start(f32[256,512]{1,0:T(8,128)} %copy-done.22) | copy-start | bytes 1572868
  388.5 58.5 %copy-start.89 = (f32[1,512]{1,0:T(1,128)S(1)}, f32[1,512]{1,0:T(1,128)}, u32[]{:S(2)}) copy-start(f32[1,512]{1,0:T(1,128)} %copy-done.88) | copy-start | bytes 6148
  388.5 58.5 %copy-start.94 = (f32[256]{0:T(256)S(1)}, f32[256]{0:T(256)}, u32[]{:S(2)}) copy-start(f32[256]{0:T(256)} %copy-done.93) | copy-start | bytes 3076
  388.6 122.4 %all-gather.25.cloned.1.call-start = ((), (), s32[]{:S(2)}) async-start(), calls=%async_computation.20 | async-start | bytes 2359296 | tf_op jit(solution)/shard_map/all_gather | solution.py:25
  461.4 180.5 %reduce-scatter.25.cloned.1.call-start = ((), (), s32[]{:S(2)}) async-start(), calls=%async_computation.21 | async-start | bytes 294912
  543.1 132.2 %reduce-scatter.27.cloned.1.call-start = ((), (), s32[]{:S(2)}) async-start(), calls=%async_computation.22 | async-start | bytes 2359296
  555.9 191.0 %reduce-scatter.21.cloned.1.call-start = ((), (), s32[]{:S(2)}) async-start(), calls=%async_computation.14 | async-start | bytes 2359296 | tf_op jit(solution)/shard_map/reduce_scatter | solution.py:313
  560.2 213.0 %reduce-scatter.19.cloned.1.call-start = ((), (), s32[]{:S(2)}) async-start(), calls=%async_computation.13 | async-start | bytes 1310720 | tf_op jit(solution)/shard_map/reduce_scatter | solution.py:278
  583.2 5.9 collective-permute-start.3
  592.1 254.0 %reduce-scatter.23.cloned.1.call-start = ((), (), s32[]{:S(2)}) async-start(), calls=%async_computation.15 | async-start | bytes 2359296 | tf_op jit(solution)/shard_map/reduce_scatter | solution.py:316
  594.8 390.2 %all-reduce.32.cloned.1.call-start = ((), (), s32[]{:S(2)}) async-start(), calls=%async_computation.16 | async-start | bytes 4194304 | tf_op jit(solution)/shard_map/psum | solution.py:329
  641.8 131.4 %copy-start.29 = (f32[256,256]{1,0:T(8,128)S(1)}, f32[256,256]{1,0:T(8,128)}, u32[]{:S(2)}) copy-start(f32[256,256]{1,0:T(8,128)} %param.25) | copy-start | bytes 786436
  641.9 131.4 %copy-start.102 = (f32[1,256]{1,0:T(1,128)S(1)}, f32[1,256]{1,0:T(1,128)}, u32[]{:S(2)}) copy-start(f32[1,256]{1,0:T(1,128)} %copy-done.101) | copy-start | bytes 3076
  641.9 131.4 %copy-start.109 = (f32[256]{0:T(256)S(1)}, f32[256]{0:T(256)}, u32[]{:S(2)}) copy-start(f32[256]{0:T(256)} %copy-done.108) | copy-start | bytes 3076
  641.9 138.2 %copy-start.123 = (f32[256]{0:T(256)S(1)}, f32[256]{0:T(256)}, u32[]{:S(2)}) copy-start(f32[256]{0:T(256)} %get-tuple-element.1182) | copy-start | bytes 3076
  641.9 176.5 %copy-start.55 = (f32[256,256]{1,0:T(8,128)S(1)}, f32[256,256]{1,0:T(8,128)}, u32[]{:S(2)}) copy-start(f32[256,256]{1,0:T(8,128)} %get-tuple-element.1264) | copy-start | bytes 786436
  (130 other events, 1273.8 us)
Sparse Core Ops, SparseCore 0:
  9.5 19.4 all-gather.14
  42.4 49.3 all-gather.18
  117.8 23.5 reduce-scatter.12
  143.4 16.6 all-gather.16
  180.7 50.1 all-gather.20
  281.7 47.2 all-gather.22
  385.8 24.1 reduce-scatter.16
  412.6 24.7 reduce-scatter.14
  461.5 49.4 all-gather.24
  543.2 60.5 reduce-scatter.24
  607.4 67.9 reduce-scatter.26
  679.3 67.6 reduce-scatter.20
  749.5 23.7 reduce-scatter.18
  776.6 69.4 reduce-scatter.22
  851.3 133.7 all-reduce.31
where the time goes:
time: 1010 us; the launch traced here: 995 us
  waiting for transfers between devices  475 us (47%)
  blocking collectives  185 us (18%)
  other arithmetic  110 us (11%)
  matrix products  100 us (10%)
  local copies, waits for them, and re-layouts  96.9 us (10%)
  between operations  17.1 us (2%)
  starting transfers between devices  10.5 us (1%)
    psum x1, waiting for transfers between devices, local(): lax.psum((stacks[11], stacks[12], stacks[13]), ('seq', 'head'))  137 us
    all_gather x4, waiting for transfers between devices, entering_2(): pieces = jax.tree.map(lambda part: lax.all_gather(part, axis), value)  94.6 us
    reduce_scatter x1, waiting for transfers between devices, local(): lax.psum_scatter(stacks[0].astype(jnp.bfloat16), 'seq', scatter_dimension...  69.4 us
    reduce_scatter x2, waiting for transfers between devices, local(): lax.psum_scatter(product(wz_now, d_gate_b) + product(wx_now, d_x_b) + pro...  45.9 us
    unnamed x2, blocking collectives  43.9 us
    reduce_scatter x2, waiting for transfers between devices, local(): lax.psum_scatter(contract_first(out_weight, scaled.T), 'head', scatter_di...  43.6 us
    psum x1, blocking collectives, local(): lax.psum((stacks[11], stacks[12], stacks[13]), ('seq', 'head'))  41.8 us
    psum x1, blocking collectives, local(): lax.psum((stacks[4], stacks[5], stacks[6], stacks[7], stacks[8], stacks[9...  38.2 us
  transfers between devices with their start and end apart: 19, of which 17 were waited for; matrix products, arithmetic and copies ran while one was open for 13% of the time, Pallas kernels for 0%

commit v1 on v0

--- a/solution.py
+++ b/solution.py
@@ -326,7 +326,7 @@
     vector_sums = lax.psum(
         (stacks[4], stacks[5], stacks[6], stacks[7], stacks[8], stacks[9], stacks[10]), "seq"
     )
-    shared_sums = lax.psum((stacks[11], stacks[12], stacks[13]), ("seq", "head"))
+    shared_sums = lax.psum(lax.psum((stacks[11], stacks[12], stacks[13]), "seq"), "head")
     return (
         hidden,
         grad,

time: 1010 us -> 1050 us (1.040)
  waiting for transfers between devices: 475 us -> 546 us
  blocking collectives: 185 us -> 149 us
    unnamed x17 -> x18, waiting for transfers between devices: 32.7 us -> 135 us
    psum x1 -> x0, blocking collectives: 41.8 us -> none  [local(): lax.psum((stacks[11], stacks[12], stacks[13]), ('seq', 'head'))]
    psum x1 -> x2, waiting for transfers between devices: 137 us -> 113 us  [the longest x1 62.1 us: local(): lax.psum((stacks[11], stacks[12], stacks[13]), 'seq')]
  transfers between devices with their start and end apart: 19 -> 20, of which waited for: 17 -> 19; matrix products, arithmetic and copies ran while one was open for 13% -> 11% of each run, Pallas kernels for 0% -> 0%
where the time goes in v1:
time: 1050 us; the launch traced here: 1030 us
  waiting for transfers between devices  546 us (52%)
  blocking collectives  149 us (14%)
  other arithmetic  116 us (11%)
  matrix products  103 us (10%)
  local copies, waits for them, and re-layouts  91.8 us (9%)
  between operations  17.1 us (2%)
    unnamed x18, waiting for transfers between devices  135 us
    all_gather x4, waiting for transfers between devices, entering_2(): pieces = jax.tree.map(lambda part: lax.all_gather(part, axis), value)  94.4 us
    reduce_scatter x1, waiting for transfers between devices, local(): lax.psum_scatter(stacks[0].astype(jnp.bfloat16), 'seq', scatter_dimension...  69.4 us
    psum x1, waiting for transfers between devices, local(): lax.psum((stacks[11], stacks[12], stacks[13]), 'seq')  62.1 us
    psum x1, waiting for transfers between devices, local(): lax.psum(lax.psum((stacks[11], stacks[12], stacks[13]), 'seq'), 'head')  50.9 us
    reduce_scatter x2, waiting for transfers between devices, local(): lax.psum_scatter(product(wz_now, d_gate_b) + product(wx_now, d_x_b) + pro...  45.8 us
    unnamed x2, blocking collectives  43.7 us
    reduce_scatter x2, waiting for transfers between devices, local(): lax.psum_scatter(contract_first(out_weight, scaled.T), 'head', scatter_di...  43.6 us
  transfers between devices with their start and end apart: 20, of which 19 were waited for; matrix products, arithmetic and copies ran while one was open for 11% of the time, Pallas kernels for 0%

profile of v1, /device:TPU:0, one launch (start us, length us, event | category | flops | bytes accessed | tf_op | source)
XLA Modules:
  0.0 1033.5 jit_solution(5410172850146453400)
XLA Ops:
  8.7 6.0 all-gather
  22.1 6.9 all-gather.15.cloned.1.call-done
  45.5 21.2 %all-reduce.26 = f32[64]{0:T(128)S(1)} all-reduce(f32[64]{0:T(128)S(1)} %exponential_dynamic-update-slice_fusion.1), channel_id=3, replica_groups=mesh['seq'=8,'head'=4] {'seq'}, use_global_device_ids=true, to_apply=%add.26 | all-reduce | flops 64 | bytes 512
  68.6 23.3 %all-gather.19.cloned.1.call-done = f32[64,64,128]{2,1,0:T(8,128)} async-done(((f32[8,64,128]{2,1,0:T(8,128)}), f32[64,64,128]{2,1,0:T(8,128)}) %all-gather.19.cloned.1.call-update) | async-done | bytes 2097168 | tf_op jit(solution)/shard_map/all_gather | solution.py:25
  91.9 7.6 while.44
  109.3 5.8 psum.133
  117.9 23.7 %reduce-scatter.13.cloned.1.call-done = f32[256,256]{0,1:T(8,128)} async-done(((f32[1024,256]{0,1:T(8,128)}), f32[256,256]{0,1:T(8,128)}) %reduce-scatter.13.cloned.1.call-update) | async-done | bytes 262160 | tf_op jit(solution)/shard_map/reduce_scatter | solution.py:179
  149.7 10.6 %all-gather.17.cloned.1.call-done = f32[256,1024]{1,0:T(8,128)} async-done(((f32[256,256]{1,0:T(8,128)}), f32[256,1024]{1,0:T(8,128)}) %all-gather.17.cloned.1.call-update) | async-done | bytes 1048592 | tf_op jit(solution)/shard_map/all_gather | solution.py:141
  181.8 7.0 all_gather.64
  189.5 22.5 %all-reduce.27 = f32[64]{0:T(128)S(1)} all-reduce(f32[64]{0:T(128)S(1)} %exponential_dynamic-update-slice_fusion), channel_id=6, replica_groups=mesh['seq'=8,'head'=4] {'seq'}, use_global_device_ids=true, to_apply=%add.27 | all-reduce | flops 64 | bytes 512
  217.7 13.3 %all-gather.21.cloned.1.call-done = f32[64,64,128]{2,1,0:T(8,128)} async-done(((f32[8,64,128]{2,1,0:T(8,128)}), f32[64,64,128]{2,1,0:T(8,128)}) %all-gather.21.cloned.1.call-update) | async-done | bytes 2097168 | tf_op jit(solution)/shard_map/all_gather | solution.py:25
  231.1 15.9 %while.45 = (s32[]{:T(128)}, f32[8,64,128]{2,1,0:T(8,128)S(1)}, s32[]{:T(128)}, f32[8,8]{1,0:T(8,128)}, f32[8,8,64,128]{3,2,1,0:T(8,128)}, /*index=5*/s32[]{:T(128)}, s32[]{:T(128)}) while((s32[]{:T(128)}, f32[8,64,128]{2,1,0:T(8,128)S(1)}, s32[]{:T(128)}, f32[8,8]{1,0:T(8,128)}, f32[8,8,64,128]{3,2,1,0:T(8,128)}, ...), condition=%wide.region_14.16_spmd.clone, body=%wide.region_13.15_spmd.clone.sunk | while | flops 262148 | bytes 786633 | solution.py:37
  267.3 6.6 psum.135
  306.6 22.5 %all-gather.23.cloned.1.call-done = f32[64,64,128]{2,1,0:T(8,128)} async-done(((f32[8,64,128]{2,1,0:T(8,128)}), f32[64,64,128]{2,1,0:T(8,128)}) %all-gather.23.cloned.1.call-update) | async-done | bytes 2097168 | tf_op jit(solution)/shard_map/all_gather | solution.py:25
  332.2 15.8 %while.46 = (s32[]{:T(128)}, f32[8,64,128]{2,1,0:T(8,128)S(1)}, s32[]{:T(128)}, f32[8,8]{1,0:T(8,128)}, f32[8,8,64,128]{3,2,1,0:T(8,128)}, /*index=5*/s32[]{:T(128)}, s32[]{:T(128)}) while((s32[]{:T(128)}, f32[8,64,128]{2,1,0:T(8,128)S(1)}, s32[]{:T(128)}, f32[8,8]{1,0:T(8,128)}, f32[8,8,64,128]{3,2,1,0:T(8,128)}, ...), condition=%wide.region_22.24_spmd.clone, body=%wide.region_21.23_spmd.clone.sunk | while | flops 262148 | bytes 786633 | solution.py:37
  359.0 12.3 %reduce-window.90 = f32[8,2,128]{2,0,1:T(8,128)S(1)} reduce-window(f32[8,2,128]{2,0,1:T(8,128)S(1)} %fusion.248, f32[]{:T(128)} %constant.312.clone.1), window={size=1x1x128 pad=0_0x0_0x0_127}, to_apply=%region_33.35 | reduce-window | flops 260096 | bytes 16388 | tf_op jit(solution)/shard_map/reduce-window.24
  398.4 21.4 %reduce-scatter.17.cloned.1.call-done = f32[256,256]{0,1:T(8,128)} async-done(((f32[1024,256]{0,1:T(8,128)}), f32[256,256]{0,1:T(8,128)}) %reduce-scatter.17.cloned.1.call-update) | async-done | bytes 262160 | tf_op jit(solution)/shard_map/reduce_scatter | solution.py:278
  427.2 19.9 %reduce-scatter.15.cloned.1.call-done = f32[256,256]{0,1:T(8,128)} async-done(((f32[1024,256]{0,1:T(8,128)}), f32[256,256]{0,1:T(8,128)}) %reduce-scatter.15.cloned.1.call-update) | async-done | bytes 262160 | tf_op jit(solution)/shard_map/reduce_scatter | solution.py:179
  449.2 6.7 all_gather.67
  459.6 6.7 psum.137
  488.4 35.3 %all-gather.25.cloned.1.call-done = f32[64,64,128]{2,1,0:T(8,128)} async-done(((f32[8,64,128]{2,1,0:T(8,128)}), f32[64,64,128]{2,1,0:T(8,128)}) %all-gather.25.cloned.1.call-update) | async-done | bytes 2097168 | tf_op jit(solution)/shard_map/all_gather | solution.py:25
  526.9 7.8 while.47
  580.9 6.2 copy.152
  603.0 62.1 %all-reduce.33.cloned.1.call-done = f32[2,1024,256]{2,1,0:T(8,128)} async-done(((f32[2,1024,256]{2,1,0:T(8,128)}), f32[2,1024,256]{2,1,0:T(8,128)}) %all-reduce.33.cloned.1.call-update) | async-done | bytes 2097168 | tf_op jit(solution)/shard_map/psum | solution.py:329
  665.2 65.2 %reduce-scatter.25.cloned.1.call-done = bf16[128,16]{1,0:T(8,128)(2,1)} async-done(((bf16[1024,16]{1,0:T(8,128)(2,1)}), bf16[128,16]{1,0:T(8,128)(2,1)}) %reduce-scatter.25.cloned.1.call-update) | async-done | bytes 4112
  731.9 69.3 %reduce-scatter.27.cloned.1.call-done = bf16[128,1024]{1,0:T(8,128)(2,1)} async-done(((bf16[1024,1024]{1,0:T(8,128)(2,1)}), bf16[128,1024]{1,0:T(8,128)(2,1)}) %reduce-scatter.27.cloned.1.call-update) | async-done | bytes 262160
  803.4 69.4 %reduce-scatter.21.cloned.1.call-done = bf16[2,128,512]{2,1,0:T(8,128)(2,1)} async-done(((bf16[2,1024,512]{2,1,0:T(8,128)(2,1)}), bf16[2,128,512]{2,1,0:T(8,128)(2,1)}) %reduce-scatter.21.cloned.1.call-update) | async-done | bytes 262160 | tf_op jit(solution)/shard_map/reduce_scatter | solution.py:313
  874.6 24.4 %reduce-scatter.19.cloned.1.call-done = f32[256,256]{0,1:T(8,128)} async-done(((f32[1024,256]{0,1:T(8,128)}), f32[256,256]{0,1:T(8,128)}) %reduce-scatter.19.cloned.1.call-update) | async-done | bytes 262160 | tf_op jit(solution)/shard_map/reduce_scatter | solution.py:278
  900.2 38.3 %all-reduce.28 = (f32[2,256]{1,0:T(2,128)}, f32[2,4,512]{2,1,0:T(4,128)}, f32[2,512]{1,0:T(2,128)}, f32[2,4,256]{2,1,0:T(4,128)S(1)}, f32[2,256]{1,0:T(2,128)S(1...) all-reduce(f32[2,256]{1,0:T(2,128)S(1)} %get-tuple-element.1335, ...), channel_id=1, replica_groups=mesh['seq'=8,'head'=4] {'seq'}, use_global_device_ids=true, to_apply=%region_62.64 | all-reduce | flops 9264 | bytes 74112 | tf_op jit(solution)/shard_map/psum | solution.py:326
  938.5 11.4 %all-reduce.29 = (f32[256]{0:T(256)S(1)}, f32[2,4,256]{2,1,0:T(4,128)}, f32[2,256]{1,0:T(2,128)}) all-reduce(f32[256]{0:T(256)S(1)} %get-tuple-element.1181, f32[2,4,256]{2,1,0:T(4,128)S(1)} %get-tuple-element.1247, f32[2,256]{1,0:T(2,128)S(1)} %get-tuple-element.1248), channel_id=1, replica_groups=mesh['seq'=8,'head'=4] {'head'}, use_global_device_ids=true, to_apply=%region_59.61 | all-reduce | flops 2816 | bytes 22528 | tf_op jit(solution)/shard_map/psum | solution.py:106
  951.7 19.1 %reduce-scatter.23.cloned.1.call-done = bf16[2,128,512]{2,1,0:T(8,128)(2,1)} async-done(((bf16[2,1024,512]{2,1,0:T(8,128)(2,1)}), bf16[2,128,512]{2,1,0:T(8,128)(2,1)}) %reduce-scatter.23.cloned.1.call-update) | async-done | bytes 262160 | tf_op jit(solution)/shard_map/reduce_scatter | solution.py:316
  972.6 50.9 %all-reduce.35.cloned.1.call-done = f32[2,1024,256]{2,1,0:T(8,128)} async-done(((f32[2,1024,256]{2,1,0:T(8,128)}), f32[2,1024,256]{2,1,0:T(8,128)}) %all-reduce.35.cloned.1.call-update) | async-done | bytes 2097168 | tf_op jit(solution)/shard_map/psum | solution.py:329
  (631 shorter events, 327.7 us)
Async XLA Ops:
  7.2 21.8 %all-gather.15.cloned.1.call-start = ((), (), s32[]{:S(2)}) async-start(), calls=%async_computation.8 | async-start | bytes 1310720 | tf_op jit(solution)/shard_map/all_gather | solution.py:141
  7.9 84.0 %all-gather.19.cloned.1.call-start = ((), (), s32[]{:S(2)}) async-start(), calls=%async_computation.18 | async-start | bytes 2359296 | tf_op jit(solution)/shard_map/all_gather | solution.py:25
  8.7 134.6 %copy-start.99 = (f32[1,256]{1,0:T(1,128)}, f32[1,256]{1,0:T(1,128)S(1)}, u32[]{:S(2)}) copy-start(f32[1,256]{1,0:T(1,128)S(1)} %get-tuple-element.1315) | copy-start | bytes 3076
  32.9 6.1 collective-permute-start
  40.4 59.1 %copy-start = (f32[256,768]{1,0:T(8,128)}, f32[256,768]{1,0:T(8,128)S(1)}, u32[]{:S(2)}) copy-start(f32[256,768]{1,0:T(8,128)S(1)} %get-tuple-element.1278) | copy-start | bytes 2359300
  40.7 59.4 %copy-start.17 = (f32[256,512]{0,1:T(8,128)}, f32[256,512]{0,1:T(8,128)S(1)}, u32[]{:S(2)}) copy-start(f32[256,512]{0,1:T(8,128)S(1)} %copy.129) | copy-start | bytes 1572868
  42.4 99.2 %reduce-scatter.13.cloned.1.call-start = ((), (), s32[]{:S(2)}) async-start(), calls=%async_computation.9 | async-start | bytes 1310720 | tf_op jit(solution)/shard_map/reduce_scatter | solution.py:179
  44.9 55.3 %copy-start.133 = (f32[8]{0:T(128)}, f32[8]{0:T(128)S(1)}, u32[]{:S(2)}) copy-start(f32[8]{0:T(128)S(1)} %get-tuple-element.1320) | copy-start | bytes 100
  45.5 69.6 %copy-start.84 = (f32[1,512]{1,0:T(1,128)}, f32[1,512]{1,0:T(1,128)S(1)}, u32[]{:S(2)}) copy-start(f32[1,512]{1,0:T(1,128)S(1)} %get-tuple-element.1310) | copy-start | bytes 6148
  117.8 42.5 %all-gather.17.cloned.1.call-start = ((), (), s32[]{:S(2)}) async-start(), calls=%async_computation.10 | async-start | bytes 1310720 | tf_op jit(solution)/shard_map/all_gather | solution.py:141
  143.3 87.7 %all-gather.21.cloned.1.call-start = ((), (), s32[]{:S(2)}) async-start(), calls=%async_computation.19 | async-start | bytes 2359296 | tf_op jit(solution)/shard_map/all_gather | solution.py:25
  167.2 4.8 collective-permute-start.1
  180.7 148.3 %all-gather.23.cloned.1.call-start = ((), (), s32[]{:S(2)}) async-start(), calls=%async_computation.20 | async-start | bytes 2359296 | tf_op jit(solution)/shard_map/all_gather | solution.py:25
  281.8 138.0 %reduce-scatter.17.cloned.1.call-start = ((), (), s32[]{:S(2)}) async-start(), calls=%async_computation.12 | async-start | bytes 1310720 | tf_op jit(solution)/shard_map/reduce_scatter | solution.py:278
  386.6 5.6 collective-permute-start.2
  395.5 51.7 %reduce-scatter.15.cloned.1.call-start = ((), (), s32[]{:S(2)}) async-start(), calls=%async_computation.11 | async-start | bytes 1310720 | tf_op jit(solution)/shard_map/reduce_scatter | solution.py:179
  398.3 58.4 %copy-start.85 = (f32[1,512]{1,0:T(1,128)S(1)}, f32[1,512]{1,0:T(1,128)}, u32[]{:S(2)}) copy-start(f32[1,512]{1,0:T(1,128)} %copy-done.84) | copy-start | bytes 6148
  398.3 58.4 %copy-start.90 = (f32[256]{0:T(256)S(1)}, f32[256]{0:T(256)}, u32[]{:S(2)}) copy-start(f32[256]{0:T(256)} %copy-done.89) | copy-start | bytes 3076
  398.4 125.3 %all-gather.25.cloned.1.call-start = ((), (), s32[]{:S(2)}) async-start(), calls=%async_computation.21 | async-start | bytes 2359296 | tf_op jit(solution)/shard_map/all_gather | solution.py:25
  474.1 191.0 %all-reduce.33.cloned.1.call-start = ((), (), s32[]{:S(2)}) async-start(), calls=%async_computation.16 | async-start | bytes 4194304 | tf_op jit(solution)/shard_map/psum | solution.py:329
  555.3 5.6 collective-permute-start.3
  563.3 167.1 %reduce-scatter.25.cloned.1.call-start = ((), (), s32[]{:S(2)}) async-start(), calls=%async_computation.22 | async-start | bytes 294912
  577.8 223.3 %reduce-scatter.27.cloned.1.call-start = ((), (), s32[]{:S(2)}) async-start(), calls=%async_computation.23 | async-start | bytes 2359296
  590.6 282.2 %reduce-scatter.21.cloned.1.call-start = ((), (), s32[]{:S(2)}) async-start(), calls=%async_computation.14 | async-start | bytes 2359296 | tf_op jit(solution)/shard_map/reduce_scatter | solution.py:313
  594.0 305.0 %reduce-scatter.19.cloned.1.call-start = ((), (), s32[]{:S(2)}) async-start(), calls=%async_computation.13 | async-start | bytes 1310720 | tf_op jit(solution)/shard_map/reduce_scatter | solution.py:278
  599.0 371.9 %reduce-scatter.23.cloned.1.call-start = ((), (), s32[]{:S(2)}) async-start(), calls=%async_computation.15 | async-start | bytes 2359296 | tf_op jit(solution)/shard_map/reduce_scatter | solution.py:316
  601.7 421.8 %all-reduce.35.cloned.1.call-start = ((), (), s32[]{:S(2)}) async-start(), calls=%async_computation.17 | async-start | bytes 4194304 | tf_op jit(solution)/shard_map/psum | solution.py:329
  665.1 233.9 %copy-start.27 = (f32[256,256]{1,0:T(8,128)S(1)}, f32[256,256]{1,0:T(8,128)}, u32[]{:S(2)}) copy-start(f32[256,256]{1,0:T(8,128)} %param.25) | copy-start | bytes 786436
  665.1 233.9 %copy-start.98 = (f32[1,256]{1,0:T(1,128)S(1)}, f32[1,256]{1,0:T(1,128)}, u32[]{:S(2)}) copy-start(f32[1,256]{1,0:T(1,128)} %copy-done.97) | copy-start | bytes 3076
  665.1 233.9 %copy-start.105 = (f32[256]{0:T(256)S(1)}, f32[256]{0:T(256)}, u32[]{:S(2)}) copy-start(f32[256]{0:T(256)} %copy-done.104) | copy-start | bytes 3076
  665.1 235.0 %copy-start.124 = (f32[256]{0:T(256)S(1)}, f32[256]{0:T(256)}, u32[]{:S(2)}) copy-start(f32[256]{0:T(256)} %get-tuple-element.1182) | copy-start | bytes 3076
  665.1 284.8 %copy-start.51 = (f32[256,256]{1,0:T(8,128)S(1)}, f32[256,256]{1,0:T(8,128)}, u32[]{:S(2)}) copy-start(f32[256,256]{1,0:T(8,128)} %get-tuple-element.1267) | copy-start | bytes 786436
  (131 other events, 1031.3 us)
Sparse Core Ops, SparseCore 0:
  9.5 19.4 all-gather.14
  42.5 49.3 all-gather.18
  118.0 23.5 reduce-scatter.12
  143.6 16.6 all-gather.16
  180.8 50.1 all-gather.20
  281.9 47.0 all-gather.22
  395.5 24.2 reduce-scatter.16
  422.3 24.7 reduce-scatter.14
  474.2 49.4 all-gather.24
  563.3 101.7 all-reduce.32
  669.0 61.3 reduce-scatter.24
  733.8 67.3 reduce-scatter.26
  805.3 67.4 reduce-scatter.20
  875.2 23.7 reduce-scatter.18
  902.4 68.4 reduce-scatter.22
  973.1 50.3 all-reduce.34
